TPU v7x, 32 devices: a whole 2x2x4 slice. The times are simulated.
32 devices in a mesh: gx: 2 (over x), gy: 4 (over z), gz: 4 (over y, core).
Axes of the slice: x: 2, y: 2, z: 4, core: 2. Of those that a mesh axis runs over, the one named last changes fastest.
Arguments:
- local_displacement: float32 [2, 4, 4, 6, 128, 128], P('gx', 'gy', 'gz'), may hold values from -6 to 6
- coarse_load: float32 [2, 4, 4, 6, 128], P('gx', 'gy', 'gz'), may hold values from -12 to 12
- flexibility: float32 [2, 4, 4, 768, 768], P('gx', 'gy', 'gz'), as said below
- block_map: int32 [2, 4, 4, 768], P('gx', 'gy', 'gz'), may hold values from 0 to 767, each once within a row
- mode_counts: int32 [2, 4, 4], P('gx', 'gy', 'gz'), may hold values from 3 to 6, as said below
- mode_traces: float32 [2, 4, 4, 6, 6, 128], P('gx', 'gy', 'gz')
- coarse_rows: float32 [2, 4, 4, 6, 192], P('gx', 'gy', 'gz'), as said below
- stored_dirs: float32 [2, 4, 4, 40, 6, 128], P('gx', 'gy', 'gz'), as said below
- stored_images: float32 [2, 4, 4, 40, 6, 128], P('gx', 'gy', 'gz'), as said below
- stored_curv: float32 [40], replicated, may hold values from 1 to 4
Outputs:
- multipliers: float32 [2, 4, 4, 6, 128, 128], P('gx', 'gy', 'gz')
- residual: float32 [2, 4, 4, 6, 128, 128], P('gx', 'gy', 'gz')
Inputs may be any that keep to these rules, and one draw needn't show every extreme that they name: `flexibility`: each subdomain's matrix is symmetric positive definite. `coarse_rows`: read as a [192, 192] matrix it is exactly symmetric: the inverse of G^T G for the coarse basis G of the present modes, with ones added on the diagonal of absent modes. `mode_counts`: modes numbered from the count on are absent. `block_map`: each subdomain's row names every interface position once. `stored_dirs`: both copies of every face agree: slot 2a of a subdomain equals slot 2a+1 of its lower neighbour along grid dimension a. `stored_images`: both copies of every face agree: slot 2a of a subdomain equals slot 2a+1 of its lower neighbour along grid dimension a.
All inputs are finite; a program needn't handle non-finite values.
Results may differ from a plain program's by a relative error of at most 0.0003.
Values sent between devices are 32-bit elements; how exact they have to be, the bound alone decides.
A program may use at most 128 MiB of HBM per device.

v0:
```python
import jax
import jax.numpy as jnp
from jax import lax
from jax.sharding import PartitionSpec as P

STORED = 40
ITERS = 3
precise = lax.Precision.HIGHEST
slot_signs = (-1.0, 1.0, -1.0, 1.0, -1.0, 1.0)


def extended(x, sides, width):
    for axis, dim in sides:
        peers, length = (lax.axis_size(axis), x.shape[dim])
        up = [(i, (i + 1) % peers) for i in range(peers)]
        down = [(j, i) for i, j in up]
        last = lax.slice_in_dim(x, length - width, length, axis=dim)
        initial = lax.slice_in_dim(x, 0, width, axis=dim)
        before = lax.ppermute(last, axis, up)
        after = lax.ppermute(initial, axis, down)
        x = jnp.concatenate([before, x, after], axis=dim)
    return x


def assemble(field):
    padded_x = extended(field[0:2], (("gx", 0),), 1)
    padded_y = extended(field[2:4], (("gy", 0),), 1)
    padded_z = extended(field[4:6], (("gz", 0),), 1)
    return jnp.stack(
        [
            field[0] + padded_x[0],
            field[1] + padded_x[3],
            field[2] + padded_y[0],
            field[3] + padded_y[3],
            field[4] + padded_z[0],
            field[5] + padded_z[3],
        ]
    )


def plus_inner(first, second):
    return jnp.sum(first[1::2] * second[1::2], axis=(0, 1))


def stored_inner(store, field):
    return jnp.einsum("isf,sfr->ir", store[:, 1::2], field[1::2], precision=precise)


def coarse_solve(loads, rows):
    return jnp.dot(
        rows, lax.all_gather(loads, ("gx", "gy", "gz"), axis=0, tiled=True), precision=precise
    )


def per_device(
    local_displacement,
    coarse_load,
    flexibility,
    block_map,
    mode_counts,
    mode_traces,
    coarse_rows,
    stored_dirs,
    stored_images,
    stored_curv,
):
    displacement = local_displacement[0, 0, 0]
    loads = coarse_load[0, 0, 0]
    flex = flexibility[0, 0, 0]
    mapping = block_map[0, 0, 0]
    rows = coarse_rows[0, 0, 0]
    dirs_store = stored_dirs[0, 0, 0]
    images_store = stored_images[0, 0, 0]
    signs = jnp.array(slot_signs, jnp.float32)
    field_signs = signs[:, None, None]
    nmodes = mode_traces.shape[3]
    present = (jnp.arange(nmodes, dtype=jnp.int32) < mode_counts[0, 0, 0]).astype(jnp.float32)
    signed = mode_traces[0, 0, 0] * present[:, None, None] * signs[None, :, None]
    size_nb = flex.shape[0]
    inverse = jnp.zeros((size_nb,), jnp.int32).at[mapping].set(jnp.arange(size_nb, dtype=jnp.int32))
    flex_face = jnp.take(jnp.take(flex, inverse, axis=0), inverse, axis=1)
    layout = displacement.shape

    def operate(field):
        flat = (field_signs * field).reshape(size_nb, layout[2])
        return jnp.dot(flex_face, flat, precision=precise).reshape(layout)

    def graph(alpha):
        return assemble(jnp.einsum("msf,mr->sfr", signed, alpha, precision=precise))

    def project(field):
        partial_loads = jnp.einsum("msf,sfr->mr", signed, field, precision=precise)
        return field - graph(coarse_solve(partial_loads, rows))

    lam = graph(coarse_solve(loads, rows))
    resid = project(assemble(field_signs * (displacement - operate(lam))))
    directions, images, curves = ([], [], [])
    for step in range(ITERS):
        local_rows = stored_inner(images_store, resid)
        if images:
            own_rows = jnp.stack([plus_inner(images[index], resid) for index in range(len(images))])
            local_rows = jnp.concatenate([local_rows, own_rows], axis=0)
        totals = lax.psum(local_rows, ("gx", "gy", "gz"))
        beta = totals[:STORED] / stored_curv[:, None]
        direction = resid - jnp.einsum("isf,ir->sfr", dirs_store, beta, precision=precise)
        for index in range(len(directions)):
            direction = direction - directions[index] * (totals[STORED + index] / curves[index])
        image_now = project(assemble(field_signs * operate(direction)))
        pair = lax.psum(
            jnp.stack([plus_inner(direction, image_now), plus_inner(direction, resid)]),
            ("gx", "gy", "gz"),
        )
        rate = pair[1] / pair[0]
        lam = lam + rate * direction
        resid = resid - rate * image_now
        directions.append(direction)
        images.append(image_now)
        curves.append(pair[0])
    return (lam[None, None, None], resid[None, None, None])


def solution(mesh):
    return jax.shard_map(
        per_device,
        mesh=mesh,
        in_specs=(
            P("gx", "gy", "gz", None, None, None),
            P("gx", "gy", "gz", None, None),
            P("gx", "gy", "gz", None, None),
            P("gx", "gy", "gz", None),
            P("gx", "gy", "gz"),
            P("gx", "gy", "gz", None, None, None),
            P("gx", "gy", "gz", None, None),
            P("gx", "gy", "gz", None, None, None),
            P("gx", "gy", "gz", None, None, None),
            P(),
        ),
        out_specs=(P("gx", "gy", "gz", None, None, None), P("gx", "gy", "gz", None, None, None)),
        check_vma=False,
    )
```

profile of v0, /device:TPU:10, one launch (start us, length us, event | category | flops | bytes accessed | tf_op | source)
XLA Modules:
  0.0 665.6 jit_solution(9631356648595068276)
XLA Ops:
  1.5 37.6 %all-gather = f32[1,1,1,192,128]{4,2,1,0,3:T(1,128)S(1)} all-gather(f32[1,1,1,6,128]{4,2,1,0,3:T(1,128)} %bitcast.275), channel_id=2, replica_groups=mesh['gx'=2,'gy'=4,'gz'=4] {'gx','gy','gz'}, dimensions={3}, use_global_device_ids=true | all-gather | bytes 101376 | tf_op jit(solution)/shard_map/all_gather | solution.py:51
  41.6 1.6 collective-permute-start
  43.9 3.4 scatter_custom_fusion
  47.3 3.5 gather_fusion
  50.8 3.3 broadcast_select_fusion
  54.1 3.0 copy.40
  57.1 5.8 gather_fusion.1
  64.3 3.3 select_bitcast_fusion
  67.7 3.1 copy.41
  71.2 4.2 collective-permute-start.3
  76.3 1.8 collective-permute-done.2
  78.9 3.7 fusion.4
  82.6 1.6 collective-permute-start.6
  84.2 2.8 collective-permute-done.6
  87.5 4.6 collective-permute-start.8
  94.2 2.1 collective-permute-done.7
  96.4 1.6 collective-permute-done.9
  99.1 37.6 %all-gather.1 = f32[32,6,128]{2,1,0:T(8,128)S(1)} all-gather(f32[1,6,128]{2,1,0:T(8,128)S(1)} %convolution_bitcast_fusion.14), channel_id=1, replica_groups=mesh['gx'=2,'gy'=4,'gz'=4] {'gx','gy','gz'}, dimensions={0}, use_global_device_ids=true | all-gather | bytes 101376 | tf_op jit(solution)/shard_map/all_gather | solution.py:51
  142.8 4.2 collective-permute-start.15
  148.4 3.0 collective-permute-done.13
  153.1 43.5 %psum.42 = f32[40,128]{1,0:T(8,128)} all-reduce(f32[40,128]{1,0:T(8,128)S(1)} %convolution_bitcast_fusion.5), channel_id=1, replica_groups=mesh['gx'=2,'gy'=4,'gz'=4] {'gx','gy','gz'}, use_global_device_ids=true, to_apply=%region_1.2 | all-reduce | flops 5120 | bytes 40960 | tf_op jit(solution)/shard_map/psum | solution.py:103
  196.6 1.8 broadcast_multiply_fusion.2
  198.4 3.7 convolution_multiply_fusion.2
  202.4 4.1 collective-permute-done.18
  209.7 3.6 collective-permute-done.19
  214.1 39.5 %all-gather.2 = f32[32,6,128]{2,1,0:T(8,128)} all-gather(f32[1,6,128]{2,1,0:T(8,128)S(1)} %convolution_bitcast_fusion.13), channel_id=1, replica_groups=mesh['gx'=2,'gy'=4,'gz'=4] {'gx','gy','gz'}, dimensions={0}, use_global_device_ids=true | all-gather | bytes 101376 | tf_op jit(solution)/shard_map/all_gather | solution.py:51
  253.6 1.6 reshape.910
  256.2 1.6 fusion.30
  259.0 1.5 constant_dynamic-update-slice_fusion.70
  260.5 1.5 constant_dynamic-update-slice_fusion.69
  262.0 1.5 constant_dynamic-update-slice_fusion.68
  263.5 1.5 constant_dynamic-update-slice_fusion.67
  265.0 1.5 constant_dynamic-update-slice_fusion.66
  267.2 4.2 collective-permute-start.27
  272.8 3.4 collective-permute-done.25
  278.5 42.5 %psum.43 = f32[2,128]{1,0:T(2,128)S(1)} all-reduce(f32[2,128]{1,0:T(2,128)S(1)} %pad_maximum_fusion.2), channel_id=1, replica_groups=mesh['gx'=2,'gy'=4,'gz'=4] {'gx','gy','gz'}, use_global_device_ids=true, to_apply=%region_4.5 | all-reduce | flops 256 | bytes 2048 | tf_op jit(solution)/shard_map/psum | solution.py:109
  324.6 39.2 %psum.44 = f32[41,128]{1,0:T(8,128)S(1)} all-reduce(f32[41,128]{1,0:T(8,128)S(1)} %pad_maximum_fusion), channel_id=1, replica_groups=mesh['gx'=2,'gy'=4,'gz'=4] {'gx','gy','gz'}, use_global_device_ids=true, to_apply=%region_6.7 | all-reduce | flops 5248 | bytes 41984 | tf_op jit(solution)/shard_map/psum | solution.py:103
  364.5 2.6 broadcast_multiply_fusion.1
  367.1 3.7 convolution_multiply_fusion.1
  371.0 4.1 collective-permute-done.30
  378.5 3.9 collective-permute-done.31
  383.3 38.7 %all-gather.3 = f32[32,6,128]{2,1,0:T(8,128)S(1)} all-gather(f32[1,6,128]{2,1,0:T(8,128)S(1)} %convolution_bitcast_fusion.12), channel_id=1, replica_groups=mesh['gx'=2,'gy'=4,'gz'=4] {'gx','gy','gz'}, dimensions={0}, use_global_device_ids=true | all-gather | bytes 101376 | tf_op jit(solution)/shard_map/all_gather | solution.py:51
  422.2 1.6 fusion.27
  429.7 1.5 constant_dynamic-update-slice_fusion.79
  431.2 1.5 constant_dynamic-update-slice_fusion.78
  433.3 4.2 collective-permute-start.39
  438.8 3.6 collective-permute-done.37
  445.1 42.5 %psum.45 = f32[2,128]{1,0:T(2,128)} all-reduce(f32[2,128]{1,0:T(2,128)} %pad_maximum_fusion.3), channel_id=1, replica_groups=mesh['gx'=2,'gy'=4,'gz'=4] {'gx','gy','gz'}, use_global_device_ids=true, to_apply=%region_9.10 | all-reduce | flops 256 | bytes 2048 | tf_op jit(solution)/shard_map/psum | solution.py:109
  491.8 39.6 %psum.46 = f32[42,128]{1,0:T(8,128)S(1)} all-reduce(f32[42,128]{1,0:T(8,128)S(1)} %pad_maximum_fusion.1), channel_id=1, replica_groups=mesh['gx'=2,'gy'=4,'gz'=4] {'gx','gy','gz'}, use_global_device_ids=true, to_apply=%region_12.13 | all-reduce | flops 5376 | bytes 43008 | tf_op jit(solution)/shard_map/psum | solution.py:103
  532.1 2.8 broadcast_multiply_fusion
  534.9 3.7 convolution_multiply_fusion
  538.9 4.1 collective-permute-done.42
  546.3 3.6 collective-permute-done.43
  550.9 38.9 %all-gather.4 = f32[32,6,128]{2,1,0:T(8,128)S(1)} all-gather(f32[1,6,128]{2,1,0:T(8,128)S(1)} %convolution_bitcast_fusion.11), channel_id=1, replica_groups=mesh['gx'=2,'gy'=4,'gz'=4] {'gx','gy','gz'}, dimensions={0}, use_global_device_ids=true | all-gather | bytes 101376 | tf_op jit(solution)/shard_map/all_gather | solution.py:51
  590.0 1.6 fusion.24
  592.9 1.5 constant_dynamic-update-slice_fusion.94
  595.9 1.5 constant_dynamic-update-slice_fusion.92
  597.4 1.5 constant_dynamic-update-slice_fusion.91
  598.9 1.5 constant_dynamic-update-slice_fusion.90
  601.0 4.2 collective-permute-start.51
  606.7 3.4 collective-permute-done.49
  611.6 42.5 %psum.47 = f32[2,128]{1,0:T(2,128)S(1)} all-reduce(f32[2,128]{1,0:T(2,128)S(1)} %pad_maximum_fusion.4), channel_id=1, replica_groups=mesh['gx'=2,'gy'=4,'gz'=4] {'gx','gy','gz'}, use_global_device_ids=true, to_apply=%region_15.16 | all-reduce | flops 256 | bytes 2048 | tf_op jit(solution)/shard_map/psum | solution.py:109
  654.2 2.1 add_bitcast_fusion
  663.7 2.0 multiply_subtract_fusion
  (424 shorter events, 72.4 us)
Async XLA Ops:
  0.6 46.7 %copy-start = (f32[1,1,1,768,768]{4,3,2,1,0:T(8,128)S(1)}, f32[1,1,1,768,768]{4,3,2,1,0:T(8,128)}, u32[]{:S(2)}) copy-start(f32[1,1,1,768,768]{4,3,2,1,0:T(8,128)} %param.13) | copy-start | bytes 7077892
  40.8 96.2 %copy-start.12 = (f32[6,6,128]{2,1,0:T(8,128)}, f32[6,6,128]{2,1,0:T(8,128)S(1)}, u32[]{:S(2)}) copy-start(f32[6,6,128]{2,1,0:T(8,128)S(1)} %fusion.16) | copy-start | bytes 55300
  41.6 21.3 %collective-permute-start = (f32[1,128,128]{2,1,0:T(8,128)S(1)}, f32[1,128,128]{2,1,0:T(8,128)}, u32[]{:S(2)}, u32[]{:S(2)}) collective-permute-start(f32[1,128,128]{2,1,0:T(8,128)S(1)} %slice.456), channel_id=1, source_target_pairs={{0,16},{16,0},{1,17},{17,1},{2,18},{18,2},{3,19},{19,3},{4,20},{20... | collective-permute-start | bytes 196616 | tf_op jit(solution)/shard_map/ppermute | solution.py:19
  63.7 11.7 %collective-permute-start.1 = (f32[1,128,128]{2,1,0:T(8,128)S(1)}, f32[1,128,128]{2,1,0:T(8,128)}, u32[]{:S(2)}, u32[]{:S(2)}) collective-permute-start(f32[1,128,128]{2,1,0:T(8,128)S(1)} %get-tuple-element.63), channel_id=1, source_target_pairs={{16,0},{0,16},{17,1},{1,17},{18,2},{2,18},{19,3},{3,19},{20,4},{4,... | collective-permute-start | bytes 196616 | tf_op jit(solution)/shard_map/ppermute | solution.py:20
  70.7 7.4 %collective-permute-start.5 = (f32[1,128,128]{2,1,0:T(8,128)S(1)}, f32[1,128,128]{2,1,0:T(8,128)S(1)}, u32[]{:S(2)}, u32[]{:S(2)}) collective-permute-start(f32[1,128,128]{2,1,0:T(8,128)S(1)} %get-tuple-element.58), channel_id=1, source_target_pairs={{1,0},{2,1},{3,2},{0,3},{5,4},{6,5},{7,6},{4,7},{9,8},{10,9},{11,1... | collective-permute-start | bytes 196616 | tf_op jit(solution)/shard_map/ppermute | solution.py:20
  70.7 7.3 %collective-permute-start.4 = (f32[1,128,128]{2,1,0:T(8,128)S(1)}, f32[1,128,128]{2,1,0:T(8,128)S(1)}, u32[]{:S(2)}, u32[]{:S(2)}) collective-permute-start(f32[1,128,128]{2,1,0:T(8,128)S(1)} %get-tuple-element.60), channel_id=1, source_target_pairs={{0,1},{1,2},{2,3},{3,0},{4,5},{5,6},{6,7},{7,4},{8,9},{9,10},{10,1... | collective-permute-start | bytes 196616 | tf_op jit(solution)/shard_map/ppermute | solution.py:19
  71.2 6.8 %collective-permute-start.2 = (f32[1,128,128]{2,1,0:T(8,128)S(1)}, f32[1,128,128]{2,1,0:T(8,128)S(1)}, u32[]{:S(2)}, u32[]{:S(2)}) collective-permute-start(f32[1,128,128]{2,1,0:T(8,128)S(1)} %get-tuple-element.61), channel_id=1, source_target_pairs={{0,4},{4,8},{8,12},{12,0},{1,5},{5,9},{9,13},{13,1},{2,6},{6,10},{... | collective-permute-start | bytes 196616 | tf_op jit(solution)/shard_map/ppermute | solution.py:19
  71.2 6.8 %collective-permute-start.3 = (f32[1,128,128]{2,1,0:T(8,128)S(1)}, f32[1,128,128]{2,1,0:T(8,128)S(1)}, u32[]{:S(2)}, u32[]{:S(2)}) collective-permute-start(f32[1,128,128]{2,1,0:T(8,128)S(1)} %get-tuple-element.62), channel_id=1, source_target_pairs={{4,0},{8,4},{12,8},{0,12},{5,1},{9,5},{13,9},{1,13},{6,2},{10,6},{... | collective-permute-start | bytes 196616 | tf_op jit(solution)/shard_map/ppermute | solution.py:20
  78.9 57.9 %copy-start.38 = (f32[1,1,1,6,192]{4,2,3,1,0:T(1,128)S(1)}, f32[1,1,1,6,192]{4,2,3,1,0:T(1,128)}, u32[]{:S(2)}) copy-start(f32[1,1,1,6,192]{4,2,3,1,0:T(1,128)} %param.17) | copy-start | bytes 13828
  82.6 4.3 collective-permute-start.6
  87.0 11.1 %collective-permute-start.11 = (f32[1,128,128]{2,1,0:T(8,128)S(1)}, f32[1,128,128]{2,1,0:T(8,128)S(1)}, u32[]{:S(2)}, u32[]{:S(2)}) collective-permute-start(f32[1,128,128]{2,1,0:T(8,128)S(1)} %get-tuple-element.52), channel_id=1, source_target_pairs={{1,0},{2,1},{3,2},{0,3},{5,4},{6,5},{7,6},{4,7},{9,8},{10,9},{11,1... | collective-permute-start | bytes 196616 | tf_op jit(solution)/shard_map/ppermute | solution.py:20
  87.0 11.0 %collective-permute-start.10 = (f32[1,128,128]{2,1,0:T(8,128)S(1)}, f32[1,128,128]{2,1,0:T(8,128)S(1)}, u32[]{:S(2)}, u32[]{:S(2)}) collective-permute-start(f32[1,128,128]{2,1,0:T(8,128)S(1)} %get-tuple-element.54), channel_id=1, source_target_pairs={{0,1},{1,2},{2,3},{3,0},{4,5},{5,6},{6,7},{7,4},{8,9},{9,10},{10,1... | collective-permute-start | bytes 196616 | tf_op jit(solution)/shard_map/ppermute | solution.py:19
  87.5 8.9 %collective-permute-start.8 = (f32[1,128,128]{2,1,0:T(8,128)S(1)}, f32[1,128,128]{2,1,0:T(8,128)S(1)}, u32[]{:S(2)}, u32[]{:S(2)}) collective-permute-start(f32[1,128,128]{2,1,0:T(8,128)S(1)} %get-tuple-element.55), channel_id=1, source_target_pairs={{0,4},{4,8},{8,12},{12,0},{1,5},{5,9},{9,13},{13,1},{2,6},{6,10},{... | collective-permute-start | bytes 196616 | tf_op jit(solution)/shard_map/ppermute | solution.py:19
  92.1 5.9 collective-permute-start.9
  92.1 4.3 collective-permute-start.7
  137.8 58.8 %copy-start.90 = (f32[40]{0:T(128)S(1)}, f32[40]{0:T(128)}, u32[]{:S(2)}) copy-start(f32[40]{0:T(128)} %param.20) | copy-start | bytes 484
  137.8 4.4 collective-permute-start.12
  142.2 9.3 %collective-permute-start.17 = (f32[1,128,128]{2,1,0:T(8,128)S(1)}, f32[1,128,128]{2,1,0:T(8,128)S(1)}, u32[]{:S(2)}, u32[]{:S(2)}) collective-permute-start(f32[1,128,128]{2,1,0:T(8,128)S(1)} %get-tuple-element.46), channel_id=1, source_target_pairs={{1,0},{2,1},{3,2},{0,3},{5,4},{6,5},{7,6},{4,7},{9,8},{10,9},{11,1... | collective-permute-start | bytes 196616 | tf_op jit(solution)/shard_map/ppermute | solution.py:20
  142.3 9.2 %collective-permute-start.16 = (f32[1,128,128]{2,1,0:T(8,128)S(1)}, f32[1,128,128]{2,1,0:T(8,128)S(1)}, u32[]{:S(2)}, u32[]{:S(2)}) collective-permute-start(f32[1,128,128]{2,1,0:T(8,128)S(1)} %get-tuple-element.48), channel_id=1, source_target_pairs={{0,1},{1,2},{2,3},{3,0},{4,5},{5,6},{6,7},{7,4},{8,9},{9,10},{10,1... | collective-permute-start | bytes 196616 | tf_op jit(solution)/shard_map/ppermute | solution.py:19
  142.8 8.6 %collective-permute-start.14 = (f32[1,128,128]{2,1,0:T(8,128)S(1)}, f32[1,128,128]{2,1,0:T(8,128)S(1)}, u32[]{:S(2)}, u32[]{:S(2)}) collective-permute-start(f32[1,128,128]{2,1,0:T(8,128)S(1)} %get-tuple-element.49), channel_id=1, source_target_pairs={{0,4},{4,8},{8,12},{12,0},{1,5},{5,9},{9,13},{13,1},{2,6},{6,10},{... | collective-permute-start | bytes 196616 | tf_op jit(solution)/shard_map/ppermute | solution.py:19
  142.8 8.7 %collective-permute-start.15 = (f32[1,128,128]{2,1,0:T(8,128)S(1)}, f32[1,128,128]{2,1,0:T(8,128)S(1)}, u32[]{:S(2)}, u32[]{:S(2)}) collective-permute-start(f32[1,128,128]{2,1,0:T(8,128)S(1)} %get-tuple-element.50), channel_id=1, source_target_pairs={{4,0},{8,4},{12,8},{0,12},{5,1},{9,5},{13,9},{1,13},{6,2},{10,6},{... | collective-permute-start | bytes 196616 | tf_op jit(solution)/shard_map/ppermute | solution.py:20
  146.9 4.4 collective-permute-start.13
  202.2 4.3 collective-permute-start.18
  206.5 7.0 %collective-permute-start.23 = (f32[1,128,128]{2,1,0:T(8,128)S(1)}, f32[1,128,128]{2,1,0:T(8,128)S(1)}, u32[]{:S(2)}, u32[]{:S(2)}) collective-permute-start(f32[1,128,128]{2,1,0:T(8,128)S(1)} %get-tuple-element.40), channel_id=1, source_target_pairs={{1,0},{2,1},{3,2},{0,3},{5,4},{6,5},{7,6},{4,7},{9,8},{10,9},{11,1... | collective-permute-start | bytes 196616 | tf_op jit(solution)/shard_map/ppermute | solution.py:20
  206.6 6.9 %collective-permute-start.22 = (f32[1,128,128]{2,1,0:T(8,128)S(1)}, f32[1,128,128]{2,1,0:T(8,128)S(1)}, u32[]{:S(2)}, u32[]{:S(2)}) collective-permute-start(f32[1,128,128]{2,1,0:T(8,128)S(1)} %get-tuple-element.42), channel_id=1, source_target_pairs={{0,1},{1,2},{2,3},{3,0},{4,5},{5,6},{6,7},{7,4},{8,9},{9,10},{10,1... | collective-permute-start | bytes 196616 | tf_op jit(solution)/shard_map/ppermute | solution.py:19
  207.1 6.3 collective-permute-start.20
  208.1 5.3 collective-permute-start.21
  209.1 4.3 collective-permute-start.19
  257.8 8.7 %collective-permute-start.24 = (f32[1,128,128]{2,1,0:T(8,128)S(1)}, f32[1,128,128]{2,1,0:T(8,128)S(1)}, u32[]{:S(2)}, u32[]{:S(2)}) collective-permute-start(f32[1,128,128]{2,1,0:T(8,128)S(1)} %slice.480), channel_id=1, source_target_pairs={{0,16},{16,0},{1,17},{17,1},{2,18},{18,2},{3,19},{19,3},{4,20},{20... | collective-permute-start | bytes 196616 | tf_op jit(solution)/shard_map/ppermute | solution.py:19
  266.6 9.8 %collective-permute-start.29 = (f32[1,128,128]{2,1,0:T(8,128)S(1)}, f32[1,128,128]{2,1,0:T(8,128)S(1)}, u32[]{:S(2)}, u32[]{:S(2)}) collective-permute-start(f32[1,128,128]{2,1,0:T(8,128)S(1)} %get-tuple-element.34), channel_id=1, source_target_pairs={{1,0},{2,1},{3,2},{0,3},{5,4},{6,5},{7,6},{4,7},{9,8},{10,9},{11,1... | collective-permute-start | bytes 196616 | tf_op jit(solution)/shard_map/ppermute | solution.py:20
  266.7 9.7 %collective-permute-start.28 = (f32[1,128,128]{2,1,0:T(8,128)S(1)}, f32[1,128,128]{2,1,0:T(8,128)S(1)}, u32[]{:S(2)}, u32[]{:S(2)}) collective-permute-start(f32[1,128,128]{2,1,0:T(8,128)S(1)} %get-tuple-element.36), channel_id=1, source_target_pairs={{0,1},{1,2},{2,3},{3,0},{4,5},{5,6},{6,7},{7,4},{8,9},{9,10},{10,1... | collective-permute-start | bytes 196616 | tf_op jit(solution)/shard_map/ppermute | solution.py:19
  267.1 9.1 %collective-permute-start.26 = (f32[1,128,128]{2,1,0:T(8,128)S(1)}, f32[1,128,128]{2,1,0:T(8,128)S(1)}, u32[]{:S(2)}, u32[]{:S(2)}) collective-permute-start(f32[1,128,128]{2,1,0:T(8,128)S(1)} %get-tuple-element.37), channel_id=1, source_target_pairs={{0,4},{4,8},{8,12},{12,0},{1,5},{5,9},{9,13},{13,1},{2,6},{6,10},{... | collective-permute-start | bytes 196616 | tf_op jit(solution)/shard_map/ppermute | solution.py:19
  267.2 9.1 %collective-permute-start.27 = (f32[1,128,128]{2,1,0:T(8,128)S(1)}, f32[1,128,128]{2,1,0:T(8,128)S(1)}, u32[]{:S(2)}, u32[]{:S(2)}) collective-permute-start(f32[1,128,128]{2,1,0:T(8,128)S(1)} %get-tuple-element.38), channel_id=1, source_target_pairs={{4,0},{8,4},{12,8},{0,12},{5,1},{9,5},{13,9},{1,13},{6,2},{10,6},{... | collective-permute-start | bytes 196616 | tf_op jit(solution)/shard_map/ppermute | solution.py:20
  271.3 4.9 collective-permute-start.25
  370.8 4.3 collective-permute-start.30
  375.2 7.3 %collective-permute-start.35 = (f32[1,128,128]{2,1,0:T(8,128)S(1)}, f32[1,128,128]{2,1,0:T(8,128)S(1)}, u32[]{:S(2)}, u32[]{:S(2)}) collective-permute-start(f32[1,128,128]{2,1,0:T(8,128)S(1)} %get-tuple-element.28), channel_id=1, source_target_pairs={{1,0},{2,1},{3,2},{0,3},{5,4},{6,5},{7,6},{4,7},{9,8},{10,9},{11,1... | collective-permute-start | bytes 196616 | tf_op jit(solution)/shard_map/ppermute | solution.py:20
  375.2 7.2 %collective-permute-start.34 = (f32[1,128,128]{2,1,0:T(8,128)S(1)}, f32[1,128,128]{2,1,0:T(8,128)S(1)}, u32[]{:S(2)}, u32[]{:S(2)}) collective-permute-start(f32[1,128,128]{2,1,0:T(8,128)S(1)} %get-tuple-element.30), channel_id=1, source_target_pairs={{0,1},{1,2},{2,3},{3,0},{4,5},{5,6},{6,7},{7,4},{8,9},{9,10},{10,1... | collective-permute-start | bytes 196616 | tf_op jit(solution)/shard_map/ppermute | solution.py:19
  375.7 6.6 collective-permute-start.32
  376.7 5.7 collective-permute-start.33
  377.8 4.5 collective-permute-start.31
  422.0 21.7 %copy-start.20 = (f32[6,128,128]{2,1,0:T(8,128)S(1)}, f32[6,128,128]{2,1,0:T(8,128)}, u32[]{:S(2)}) copy-start(f32[6,128,128]{2,1,0:T(8,128)} %copy-done.19) | copy-start | bytes 1179652
  422.2 21.6 %copy-start.9 = (f32[6,128,128]{2,1,0:T(8,128)S(1)}, f32[6,128,128]{2,1,0:T(8,128)}, u32[]{:S(2)}) copy-start(f32[6,128,128]{2,1,0:T(8,128)} %get-tuple-element.69) | copy-start | bytes 1179652
  423.8 8.9 %collective-permute-start.36 = (f32[1,128,128]{2,1,0:T(8,128)S(1)}, f32[1,128,128]{2,1,0:T(8,128)S(1)}, u32[]{:S(2)}, u32[]{:S(2)}) collective-permute-start(f32[1,128,128]{2,1,0:T(8,128)S(1)} %slice.494), channel_id=1, source_target_pairs={{0,16},{16,0},{1,17},{17,1},{2,18},{18,2},{3,19},{19,3},{4,20},{20... | collective-permute-start | bytes 196616 | tf_op jit(solution)/shard_map/ppermute | solution.py:19
  432.7 9.8 %collective-permute-start.41 = (f32[1,128,128]{2,1,0:T(8,128)S(1)}, f32[1,128,128]{2,1,0:T(8,128)S(1)}, u32[]{:S(2)}, u32[]{:S(2)}) collective-permute-start(f32[1,128,128]{2,1,0:T(8,128)S(1)} %get-tuple-element.22), channel_id=1, source_target_pairs={{1,0},{2,1},{3,2},{0,3},{5,4},{6,5},{7,6},{4,7},{9,8},{10,9},{11,1... | collective-permute-start | bytes 196616 | tf_op jit(solution)/shard_map/ppermute | solution.py:20
  432.8 9.7 %collective-permute-start.40 = (f32[1,128,128]{2,1,0:T(8,128)S(1)}, f32[1,128,128]{2,1,0:T(8,128)S(1)}, u32[]{:S(2)}, u32[]{:S(2)}) collective-permute-start(f32[1,128,128]{2,1,0:T(8,128)S(1)} %get-tuple-element.24), channel_id=1, source_target_pairs={{0,1},{1,2},{2,3},{3,0},{4,5},{5,6},{6,7},{7,4},{8,9},{9,10},{10,1... | collective-permute-start | bytes 196616 | tf_op jit(solution)/shard_map/ppermute | solution.py:19
  433.3 9.1 %collective-permute-start.38 = (f32[1,128,128]{2,1,0:T(8,128)S(1)}, f32[1,128,128]{2,1,0:T(8,128)S(1)}, u32[]{:S(2)}, u32[]{:S(2)}) collective-permute-start(f32[1,128,128]{2,1,0:T(8,128)S(1)} %get-tuple-element.25), channel_id=1, source_target_pairs={{0,4},{4,8},{8,12},{12,0},{1,5},{5,9},{9,13},{13,1},{2,6},{6,10},{... | collective-permute-start | bytes 196616 | tf_op jit(solution)/shard_map/ppermute | solution.py:19
  433.3 9.1 %collective-permute-start.39 = (f32[1,128,128]{2,1,0:T(8,128)S(1)}, f32[1,128,128]{2,1,0:T(8,128)S(1)}, u32[]{:S(2)}, u32[]{:S(2)}) collective-permute-start(f32[1,128,128]{2,1,0:T(8,128)S(1)} %get-tuple-element.26), channel_id=1, source_target_pairs={{4,0},{8,4},{12,8},{0,12},{5,1},{9,5},{13,9},{1,13},{6,2},{10,6},{... | collective-permute-start | bytes 196616 | tf_op jit(solution)/shard_map/ppermute | solution.py:20
  437.4 4.9 collective-permute-start.37
  538.7 4.3 collective-permute-start.42
  543.0 7.1 %collective-permute-start.47 = (f32[1,128,128]{2,1,0:T(8,128)S(1)}, f32[1,128,128]{2,1,0:T(8,128)S(1)}, u32[]{:S(2)}, u32[]{:S(2)}) collective-permute-start(f32[1,128,128]{2,1,0:T(8,128)S(1)} %get-tuple-element.16), channel_id=1, source_target_pairs={{1,0},{2,1},{3,2},{0,3},{5,4},{6,5},{7,6},{4,7},{9,8},{10,9},{11,1... | collective-permute-start | bytes 196616 | tf_op jit(solution)/shard_map/ppermute | solution.py:20
  543.1 7.0 %collective-permute-start.46 = (f32[1,128,128]{2,1,0:T(8,128)S(1)}, f32[1,128,128]{2,1,0:T(8,128)S(1)}, u32[]{:S(2)}, u32[]{:S(2)}) collective-permute-start(f32[1,128,128]{2,1,0:T(8,128)S(1)} %get-tuple-element.18), channel_id=1, source_target_pairs={{0,1},{1,2},{2,3},{3,0},{4,5},{5,6},{6,7},{7,4},{8,9},{9,10},{10,1... | collective-permute-start | bytes 196616 | tf_op jit(solution)/shard_map/ppermute | solution.py:19
  543.6 6.4 collective-permute-start.44
  544.6 5.4 collective-permute-start.45
  545.7 4.3 collective-permute-start.43
  589.9 21.6 %copy-start.22 = (f32[6,128,128]{2,1,0:T(8,128)S(1)}, f32[6,128,128]{2,1,0:T(8,128)}, u32[]{:S(2)}) copy-start(f32[6,128,128]{2,1,0:T(8,128)} %copy-done.21) | copy-start | bytes 1179652
  591.7 62.4 %copy-start.10 = (f32[6,128,128]{2,1,0:T(8,128)S(1)}, f32[6,128,128]{2,1,0:T(8,128)}, u32[]{:S(2)}) copy-start(f32[6,128,128]{2,1,0:T(8,128)} %get-tuple-element.69) | copy-start | bytes 1179652
  591.7 62.4 %copy-start.92 = (f32[128]{0:T(128)S(1)}, f32[128]{0:T(128)}, u32[]{:S(2)}) copy-start(f32[128]{0:T(128)} %copy-done.91) | copy-start | bytes 1540
  591.7 62.4 %copy-start.94 = (f32[128]{0:T(128)S(1)}, f32[128]{0:T(128)}, u32[]{:S(2)}) copy-start(f32[128]{0:T(128)} %copy-done.93) | copy-start | bytes 1540
  591.7 8.7 %collective-permute-start.48 = (f32[1,128,128]{2,1,0:T(8,128)S(1)}, f32[1,128,128]{2,1,0:T(8,128)S(1)}, u32[]{:S(2)}, u32[]{:S(2)}) collective-permute-start(f32[1,128,128]{2,1,0:T(8,128)S(1)} %slice.509), channel_id=1, source_target_pairs={{0,16},{16,0},{1,17},{17,1},{2,18},{18,2},{3,19},{19,3},{4,20},{20... | collective-permute-start | bytes 196616 | tf_op jit(solution)/shard_map/ppermute | solution.py:19
  600.4 9.8 %collective-permute-start.53 = (f32[1,128,128]{2,1,0:T(8,128)S(1)}, f32[1,128,128]{2,1,0:T(8,128)S(1)}, u32[]{:S(2)}, u32[]{:S(2)}) collective-permute-start(f32[1,128,128]{2,1,0:T(8,128)S(1)} %get-tuple-element.10), channel_id=1, source_target_pairs={{1,0},{2,1},{3,2},{0,3},{5,4},{6,5},{7,6},{4,7},{9,8},{10,9},{11,1... | collective-permute-start | bytes 196616 | tf_op jit(solution)/shard_map/ppermute | solution.py:20
  600.5 9.7 %collective-permute-start.52 = (f32[1,128,128]{2,1,0:T(8,128)S(1)}, f32[1,128,128]{2,1,0:T(8,128)S(1)}, u32[]{:S(2)}, u32[]{:S(2)}) collective-permute-start(f32[1,128,128]{2,1,0:T(8,128)S(1)} %get-tuple-element.12), channel_id=1, source_target_pairs={{0,1},{1,2},{2,3},{3,0},{4,5},{5,6},{6,7},{7,4},{8,9},{9,10},{10,1... | collective-permute-start | bytes 196616 | tf_op jit(solution)/shard_map/ppermute | solution.py:19
  601.0 9.1 %collective-permute-start.50 = (f32[1,128,128]{2,1,0:T(8,128)S(1)}, f32[1,128,128]{2,1,0:T(8,128)S(1)}, u32[]{:S(2)}, u32[]{:S(2)}) collective-permute-start(f32[1,128,128]{2,1,0:T(8,128)S(1)} %get-tuple-element.13), channel_id=1, source_target_pairs={{0,4},{4,8},{8,12},{12,0},{1,5},{5,9},{9,13},{13,1},{2,6},{6,10},{... | collective-permute-start | bytes 196616 | tf_op jit(solution)/shard_map/ppermute | solution.py:19
  601.0 9.1 %collective-permute-start.51 = (f32[1,128,128]{2,1,0:T(8,128)S(1)}, f32[1,128,128]{2,1,0:T(8,128)S(1)}, u32[]{:S(2)}, u32[]{:S(2)}) collective-permute-start(f32[1,128,128]{2,1,0:T(8,128)S(1)} %get-tuple-element.14), channel_id=1, source_target_pairs={{4,0},{8,4},{12,8},{0,12},{5,1},{9,5},{13,9},{1,13},{6,2},{10,6},{... | collective-permute-start | bytes 196616 | tf_op jit(solution)/shard_map/ppermute | solution.py:20
  605.2 4.9 collective-permute-start.49
  (86 other events, 424.6 us)
where the time goes:
time: 668 us; the launch traced here: 666 us
  blocking collectives  442 us (66%)
  other arithmetic  60.4 us (9%)
  starting transfers between devices  49.7 us (7%)
  waiting for transfers between devices  45.8 us (7%)
  matrix products  34.5 us (5%)
  local copies, waits for them, and re-layouts  29.8 us (4%)
    all_gather x5, blocking collectives, coarse_solve(): lax.all_gather(loads, ('gx', 'gy', 'gz'), axis=0, tiled=True)  192 us
    psum x3, blocking collectives, per_device(): lax.psum(jnp.stack([plus_inner(direction, image_now), plus_inner(directio...  127 us
    psum x3, blocking collectives, per_device(): totals = lax.psum(local_rows, ('gx', 'gy', 'gz'))  122 us
    unnamed x76, other arithmetic  32.8 us
    ppermute x27, starting transfers between devices, extended(): after = lax.ppermute(initial, axis, down)  29.9 us
    ppermute x27, waiting for transfers between devices, extended(): after = lax.ppermute(initial, axis, down)  28.2 us
    ppermute x27, starting transfers between devices, extended(): before = lax.ppermute(last, axis, up)  19.8 us
    ppermute x27, waiting for transfers between devices, extended(): before = lax.ppermute(last, axis, up)  17.5 us
  transfers between devices with their start and end apart: 54, of which 15 were waited for; matrix products, arithmetic and copies ran while one was open for 9% of the time, Pallas kernels for 0%

commit v1 on v0

--- a/solution.py
+++ b/solution.py
@@ -100,7 +100,7 @@
         if images:
             own_rows = jnp.stack([plus_inner(images[index], resid) for index in range(len(images))])
             local_rows = jnp.concatenate([local_rows, own_rows], axis=0)
-        totals = lax.psum(local_rows, ("gx", "gy", "gz"))
+        totals = lax.psum(lax.psum(local_rows, ("gy", "gz")), "gx")
         beta = totals[:STORED] / stored_curv[:, None]
         direction = resid - jnp.einsum("isf,ir->sfr", dirs_store, beta, precision=precise)
         for index in range(len(directions)):

time: 668 us -> 740 us (1.11)
  blocking collectives: 442 us -> 494 us
  starting transfers between devices: 49.7 us -> 77.5 us
  waiting for transfers between devices: 45.8 us -> 34.4 us
    psum x3 -> x6, blocking collectives: 122 us -> 177 us  [per_device(): totals = lax.psum(lax.psum(local_rows, ('gy', 'gz')), 'gx')]
    ppermute x27, starting transfers between devices: 29.9 us -> 60.6 us  [extended(): after = lax.ppermute(initial, axis, down)]
  transfers between devices with their start and end apart: 54 -> 54, of which waited for: 15 -> 14; matrix products, arithmetic and copies ran while one was open for 9% -> 8% of each run, Pallas kernels for 0% -> 0%
where the time goes in v1:
time: 740 us; the launch traced here: 738 us
  blocking collectives  494 us (67%)
  starting transfers between devices  77.5 us (10%)
  other arithmetic  64.4 us (9%)
  matrix products  34.5 us (5%)
  waiting for transfers between devices  34.4 us (5%)
  local copies, waits for them, and re-layouts  29.9 us (4%)
    all_gather x5, blocking collectives, coarse_solve(): lax.all_gather(loads, ('gx', 'gy', 'gz'), axis=0, tiled=True)  187 us
    psum x6, blocking collectives, per_device(): totals = lax.psum(lax.psum(local_rows, ('gy', 'gz')), 'gx')  177 us
    psum x3, blocking collectives, per_device(): lax.psum(jnp.stack([plus_inner(direction, image_now), plus_inner(directio...  130 us
    ppermute x27, starting transfers between devices, extended(): after = lax.ppermute(initial, axis, down)  60.6 us
    unnamed x76, other arithmetic  36.1 us
    ppermute x27, waiting for transfers between devices, extended(): after = lax.ppermute(initial, axis, down)  22.5 us
    ppermute x27, starting transfers between devices, extended(): before = lax.ppermute(last, axis, up)  17 us
    dot_general x4, matrix products, operate(): return jnp.dot(flex_face, flat, precision=precise).reshape(layout)  14.8 us
  transfers between devices with their start and end apart: 54, of which 14 were waited for; matrix products, arithmetic and copies ran while one was open for 8% of the time, Pallas kernels for 0%

profile of v1, /device:TPU:10, one launch (start us, length us, event | category | flops | bytes accessed | tf_op | source)
XLA Modules:
  0.0 737.6 jit_solution(11555076397813237771)
XLA Ops:
  1.5 37.6 %all-gather = f32[1,1,1,192,128]{4,2,1,0,3:T(1,128)S(1)} all-gather(f32[1,1,1,6,128]{4,2,1,0,3:T(1,128)} %bitcast.275), channel_id=2, replica_groups=mesh['gx'=2,'gy'=4,'gz'=4] {'gx','gy','gz'}, dimensions={3}, use_global_device_ids=true | all-gather | bytes 101376 | tf_op jit(solution)/shard_map/all_gather | solution.py:51
  41.6 1.6 collective-permute-start
  43.9 3.4 scatter_custom_fusion
  47.3 3.5 gather_fusion
  50.8 3.3 broadcast_select_fusion
  54.1 3.0 copy.40
  57.1 5.7 gather_fusion.1
  64.3 3.3 select_bitcast_fusion
  67.6 3.1 copy.41
  71.2 4.2 collective-permute-start.3
  76.2 1.8 collective-permute-done.2
  78.8 3.7 fusion.4
  82.5 1.6 collective-permute-start.6
  84.1 2.8 collective-permute-done.6
  87.5 4.6 collective-permute-start.8
  94.2 2.2 collective-permute-done.7
  96.4 1.6 collective-permute-done.9
  99.1 37.6 %all-gather.1 = f32[32,6,128]{2,1,0:T(8,128)S(1)} all-gather(f32[1,6,128]{2,1,0:T(8,128)S(1)} %convolution_bitcast_fusion.14), channel_id=1, replica_groups=mesh['gx'=2,'gy'=4,'gz'=4] {'gx','gy','gz'}, dimensions={0}, use_global_device_ids=true | all-gather | bytes 101376 | tf_op jit(solution)/shard_map/all_gather | solution.py:51
  142.7 4.2 collective-permute-start.15
  148.4 3.0 collective-permute-done.13
  153.0 54.6 %psum.63 = f32[40,128]{1,0:T(8,128)S(1)} all-reduce(f32[40,128]{1,0:T(8,128)S(1)} %convolution_bitcast_fusion.5), channel_id=1, replica_groups=mesh['gx'=2,'gy'=4,'gz'=4] {'gy','gz'}, use_global_device_ids=true, to_apply=%region_1.2 | all-reduce | flops 5120 | bytes 40960 | tf_op jit(solution)/shard_map/psum | solution.py:103
  207.6 7.6 %psum.64 = f32[40,128]{1,0:T(8,128)} all-reduce(f32[40,128]{1,0:T(8,128)S(1)} %psum.63), channel_id=1, replica_groups=mesh['gx'=2,'gy'=4,'gz'=4] {'gx'}, use_global_device_ids=true, to_apply=%region_2.3 | all-reduce | flops 5120 | bytes 40960 | tf_op jit(solution)/shard_map/psum | solution.py:103
  215.2 1.8 broadcast_multiply_fusion.2
  217.0 3.7 convolution_multiply_fusion.2
  220.8 1.8 collective-permute-start.18
  227.2 8.4 %collective-permute-start.21 = (f32[1,128,128]{2,1,0:T(8,128)S(1)}, f32[1,128,128]{2,1,0:T(8,128)S(1)}, u32[]{:S(2)}, u32[]{:S(2)}) collective-permute-start(f32[1,128,128]{2,1,0:T(8,128)S(1)} %get-tuple-element.44), channel_id=1, source_target_pairs={{4,0},{8,4},{12,8},{0,12},{5,1},{9,5},{13,9},{1,13},{6,2},{10,6},{... | collective-permute-start | bytes 196616 | tf_op jit(solution)/shard_map/ppermute | solution.py:20
  236.5 3.4 collective-permute-done.19
  240.7 39.0 %all-gather.2 = f32[32,6,128]{2,1,0:T(8,128)} all-gather(f32[1,6,128]{2,1,0:T(8,128)S(1)} %convolution_bitcast_fusion.13), channel_id=1, replica_groups=mesh['gx'=2,'gy'=4,'gz'=4] {'gx','gy','gz'}, dimensions={0}, use_global_device_ids=true | all-gather | bytes 101376 | tf_op jit(solution)/shard_map/all_gather | solution.py:51
  279.7 1.6 reshape.910
  282.3 1.6 fusion.30
  291.7 1.8 collective-permute-start.29
  293.5 4.2 collective-permute-start.27
  297.7 1.7 collective-permute-start.25
  300.0 2.0 collective-permute-done.25
  304.2 43.4 %psum.65 = f32[2,128]{1,0:T(2,128)S(1)} all-reduce(f32[2,128]{1,0:T(2,128)S(1)} %pad_maximum_fusion.2), channel_id=1, replica_groups=mesh['gx'=2,'gy'=4,'gz'=4] {'gx','gy','gz'}, use_global_device_ids=true, to_apply=%region_5.6 | all-reduce | flops 256 | bytes 2048 | tf_op jit(solution)/shard_map/psum | solution.py:109
  351.4 49.3 %psum.66 = f32[41,128]{1,0:T(8,128)S(1)} all-reduce(f32[41,128]{1,0:T(8,128)S(1)} %pad_maximum_fusion), channel_id=1, replica_groups=mesh['gx'=2,'gy'=4,'gz'=4] {'gy','gz'}, use_global_device_ids=true, to_apply=%region_7.8 | all-reduce | flops 5248 | bytes 41984 | tf_op jit(solution)/shard_map/psum | solution.py:103
  400.7 8.0 %psum.67 = f32[41,128]{1,0:T(8,128)S(1)} all-reduce(f32[41,128]{1,0:T(8,128)S(1)} %psum.66), channel_id=1, replica_groups=mesh['gx'=2,'gy'=4,'gz'=4] {'gx'}, use_global_device_ids=true, to_apply=%region_8.9 | all-reduce | flops 5248 | bytes 41984 | tf_op jit(solution)/shard_map/psum | solution.py:103
  409.3 2.6 broadcast_multiply_fusion.1
  411.9 3.7 convolution_multiply_fusion.1
  416.7 3.3 collective-permute-done.30
  420.6 8.4 %collective-permute-start.33 = (f32[1,128,128]{2,1,0:T(8,128)S(1)}, f32[1,128,128]{2,1,0:T(8,128)S(1)}, u32[]{:S(2)}, u32[]{:S(2)}) collective-permute-start(f32[1,128,128]{2,1,0:T(8,128)S(1)} %get-tuple-element.32), channel_id=1, source_target_pairs={{4,0},{8,4},{12,8},{0,12},{5,1},{9,5},{13,9},{1,13},{6,2},{10,6},{... | collective-permute-start | bytes 196616 | tf_op jit(solution)/shard_map/ppermute | solution.py:20
  430.5 2.8 collective-permute-done.31
  434.2 36.5 %all-gather.3 = f32[32,6,128]{2,1,0:T(8,128)S(1)} all-gather(f32[1,6,128]{2,1,0:T(8,128)S(1)} %convolution_bitcast_fusion.12), channel_id=1, replica_groups=mesh['gx'=2,'gy'=4,'gz'=4] {'gx','gy','gz'}, dimensions={0}, use_global_device_ids=true | all-gather | bytes 101376 | tf_op jit(solution)/shard_map/all_gather | solution.py:51
  471.0 1.6 fusion.27
  481.0 1.7 collective-permute-start.41
  482.7 4.2 collective-permute-start.39
  488.7 2.4 collective-permute-done.37
  493.9 43.3 %psum.68 = f32[2,128]{1,0:T(2,128)} all-reduce(f32[2,128]{1,0:T(2,128)} %pad_maximum_fusion.3), channel_id=1, replica_groups=mesh['gx'=2,'gy'=4,'gz'=4] {'gx','gy','gz'}, use_global_device_ids=true, to_apply=%region_11.12 | all-reduce | flops 256 | bytes 2048 | tf_op jit(solution)/shard_map/psum | solution.py:109
  541.4 49.4 %psum.69 = f32[42,128]{1,0:T(8,128)S(1)} all-reduce(f32[42,128]{1,0:T(8,128)S(1)} %pad_maximum_fusion.1), channel_id=1, replica_groups=mesh['gx'=2,'gy'=4,'gz'=4] {'gy','gz'}, use_global_device_ids=true, to_apply=%region_14.15 | all-reduce | flops 5376 | bytes 43008 | tf_op jit(solution)/shard_map/psum | solution.py:103
  590.8 8.0 %psum.70 = f32[42,128]{1,0:T(8,128)S(1)} all-reduce(f32[42,128]{1,0:T(8,128)S(1)} %psum.69), channel_id=1, replica_groups=mesh['gx'=2,'gy'=4,'gz'=4] {'gx'}, use_global_device_ids=true, to_apply=%region_15.16 | all-reduce | flops 5376 | bytes 43008 | tf_op jit(solution)/shard_map/psum | solution.py:103
  599.5 2.8 broadcast_multiply_fusion
  602.3 3.7 convolution_multiply_fusion
  607.1 3.3 collective-permute-done.42
  611.0 8.5 %collective-permute-start.45 = (f32[1,128,128]{2,1,0:T(8,128)S(1)}, f32[1,128,128]{2,1,0:T(8,128)S(1)}, u32[]{:S(2)}, u32[]{:S(2)}) collective-permute-start(f32[1,128,128]{2,1,0:T(8,128)S(1)} %get-tuple-element.20), channel_id=1, source_target_pairs={{4,0},{8,4},{12,8},{0,12},{5,1},{9,5},{13,9},{1,13},{6,2},{10,6},{... | collective-permute-start | bytes 196616 | tf_op jit(solution)/shard_map/ppermute | solution.py:20
  620.9 2.8 collective-permute-done.43
  624.7 36.3 %all-gather.4 = f32[32,6,128]{2,1,0:T(8,128)S(1)} all-gather(f32[1,6,128]{2,1,0:T(8,128)S(1)} %convolution_bitcast_fusion.11), channel_id=1, replica_groups=mesh['gx'=2,'gy'=4,'gz'=4] {'gx','gy','gz'}, dimensions={0}, use_global_device_ids=true | all-gather | bytes 101376 | tf_op jit(solution)/shard_map/all_gather | solution.py:51
  661.2 1.6 fusion.24
  668.2 1.5 constant_dynamic-update-slice_fusion.91
  671.3 1.7 collective-permute-start.53
  673.0 4.2 collective-permute-start.51
  679.0 2.4 collective-permute-done.49
  683.0 43.1 %psum.71 = f32[2,128]{1,0:T(2,128)S(1)} all-reduce(f32[2,128]{1,0:T(2,128)S(1)} %pad_maximum_fusion.4), channel_id=1, replica_groups=mesh['gx'=2,'gy'=4,'gz'=4] {'gx','gy','gz'}, use_global_device_ids=true, to_apply=%region_18.19 | all-reduce | flops 256 | bytes 2048 | tf_op jit(solution)/shard_map/psum | solution.py:109
  726.1 2.1 add_bitcast_fusion
  735.6 2.0 multiply_subtract_fusion
  (421 shorter events, 85.3 us)
Async XLA Ops:
  0.6 46.7 %copy-start = (f32[1,1,1,768,768]{4,3,2,1,0:T(8,128)S(1)}, f32[1,1,1,768,768]{4,3,2,1,0:T(8,128)}, u32[]{:S(2)}) copy-start(f32[1,1,1,768,768]{4,3,2,1,0:T(8,128)} %param.13) | copy-start | bytes 7077892
  40.8 96.1 %copy-start.12 = (f32[6,6,128]{2,1,0:T(8,128)}, f32[6,6,128]{2,1,0:T(8,128)S(1)}, u32[]{:S(2)}) copy-start(f32[6,6,128]{2,1,0:T(8,128)S(1)} %fusion.16) | copy-start | bytes 55300
  41.6 21.3 %collective-permute-start = (f32[1,128,128]{2,1,0:T(8,128)S(1)}, f32[1,128,128]{2,1,0:T(8,128)}, u32[]{:S(2)}, u32[]{:S(2)}) collective-permute-start(f32[1,128,128]{2,1,0:T(8,128)S(1)} %slice.456), channel_id=1, source_target_pairs={{0,16},{16,0},{1,17},{17,1},{2,18},{18,2},{3,19},{19,3},{4,20},{20... | collective-permute-start | bytes 196616 | tf_op jit(solution)/shard_map/ppermute | solution.py:19
  63.7 11.6 %collective-permute-start.1 = (f32[1,128,128]{2,1,0:T(8,128)S(1)}, f32[1,128,128]{2,1,0:T(8,128)}, u32[]{:S(2)}, u32[]{:S(2)}) collective-permute-start(f32[1,128,128]{2,1,0:T(8,128)S(1)} %get-tuple-element.63), channel_id=1, source_target_pairs={{16,0},{0,16},{17,1},{1,17},{18,2},{2,18},{19,3},{3,19},{20,4},{4,... | collective-permute-start | bytes 196616 | tf_op jit(solution)/shard_map/ppermute | solution.py:20
  70.7 7.4 collective-permute-start.5
  70.7 7.3 collective-permute-start.4
  71.2 6.8 collective-permute-start.2
  71.2 6.8 collective-permute-start.3
  78.8 57.9 %copy-start.36 = (f32[1,1,1,6,192]{4,2,3,1,0:T(1,128)S(1)}, f32[1,1,1,6,192]{4,2,3,1,0:T(1,128)}, u32[]{:S(2)}) copy-start(f32[1,1,1,6,192]{4,2,3,1,0:T(1,128)} %param.17) | copy-start | bytes 13828
  82.5 4.3 collective-permute-start.6
  86.9 11.1 %collective-permute-start.11 = (f32[1,128,128]{2,1,0:T(8,128)S(1)}, f32[1,128,128]{2,1,0:T(8,128)S(1)}, u32[]{:S(2)}, u32[]{:S(2)}) collective-permute-start(f32[1,128,128]{2,1,0:T(8,128)S(1)} %get-tuple-element.52), channel_id=1, source_target_pairs={{1,0},{2,1},{3,2},{0,3},{5,4},{6,5},{7,6},{4,7},{9,8},{10,9},{11,1... | collective-permute-start | bytes 196616 | tf_op jit(solution)/shard_map/ppermute | solution.py:20
  87.0 11.0 %collective-permute-start.10 = (f32[1,128,128]{2,1,0:T(8,128)S(1)}, f32[1,128,128]{2,1,0:T(8,128)S(1)}, u32[]{:S(2)}, u32[]{:S(2)}) collective-permute-start(f32[1,128,128]{2,1,0:T(8,128)S(1)} %get-tuple-element.54), channel_id=1, source_target_pairs={{0,1},{1,2},{2,3},{3,0},{4,5},{5,6},{6,7},{7,4},{8,9},{9,10},{10,1... | collective-permute-start | bytes 196616 | tf_op jit(solution)/shard_map/ppermute | solution.py:19
  87.5 8.9 %collective-permute-start.8 = (f32[1,128,128]{2,1,0:T(8,128)S(1)}, f32[1,128,128]{2,1,0:T(8,128)S(1)}, u32[]{:S(2)}, u32[]{:S(2)}) collective-permute-start(f32[1,128,128]{2,1,0:T(8,128)S(1)} %get-tuple-element.55), channel_id=1, source_target_pairs={{0,4},{4,8},{8,12},{12,0},{1,5},{5,9},{9,13},{13,1},{2,6},{6,10},{... | collective-permute-start | bytes 196616 | tf_op jit(solution)/shard_map/ppermute | solution.py:19
  92.1 5.9 collective-permute-start.9
  92.1 4.3 collective-permute-start.7
  137.7 77.5 %copy-start.87 = (f32[40]{0:T(128)S(1)}, f32[40]{0:T(128)}, u32[]{:S(2)}) copy-start(f32[40]{0:T(128)} %param.20) | copy-start | bytes 484
  137.7 4.4 collective-permute-start.12
  142.2 9.3 %collective-permute-start.17 = (f32[1,128,128]{2,1,0:T(8,128)S(1)}, f32[1,128,128]{2,1,0:T(8,128)S(1)}, u32[]{:S(2)}, u32[]{:S(2)}) collective-permute-start(f32[1,128,128]{2,1,0:T(8,128)S(1)} %get-tuple-element.46), channel_id=1, source_target_pairs={{1,0},{2,1},{3,2},{0,3},{5,4},{6,5},{7,6},{4,7},{9,8},{10,9},{11,1... | collective-permute-start | bytes 196616 | tf_op jit(solution)/shard_map/ppermute | solution.py:20
  142.2 9.2 %collective-permute-start.16 = (f32[1,128,128]{2,1,0:T(8,128)S(1)}, f32[1,128,128]{2,1,0:T(8,128)S(1)}, u32[]{:S(2)}, u32[]{:S(2)}) collective-permute-start(f32[1,128,128]{2,1,0:T(8,128)S(1)} %get-tuple-element.48), channel_id=1, source_target_pairs={{0,1},{1,2},{2,3},{3,0},{4,5},{5,6},{6,7},{7,4},{8,9},{9,10},{10,1... | collective-permute-start | bytes 196616 | tf_op jit(solution)/shard_map/ppermute | solution.py:19
  142.7 8.6 %collective-permute-start.14 = (f32[1,128,128]{2,1,0:T(8,128)S(1)}, f32[1,128,128]{2,1,0:T(8,128)S(1)}, u32[]{:S(2)}, u32[]{:S(2)}) collective-permute-start(f32[1,128,128]{2,1,0:T(8,128)S(1)} %get-tuple-element.49), channel_id=1, source_target_pairs={{0,4},{4,8},{8,12},{12,0},{1,5},{5,9},{9,13},{13,1},{2,6},{6,10},{... | collective-permute-start | bytes 196616 | tf_op jit(solution)/shard_map/ppermute | solution.py:19
  142.7 8.7 %collective-permute-start.15 = (f32[1,128,128]{2,1,0:T(8,128)S(1)}, f32[1,128,128]{2,1,0:T(8,128)S(1)}, u32[]{:S(2)}, u32[]{:S(2)}) collective-permute-start(f32[1,128,128]{2,1,0:T(8,128)S(1)} %get-tuple-element.50), channel_id=1, source_target_pairs={{4,0},{8,4},{12,8},{0,12},{5,1},{9,5},{13,9},{1,13},{6,2},{10,6},{... | collective-permute-start | bytes 196616 | tf_op jit(solution)/shard_map/ppermute | solution.py:20
  146.9 4.4 collective-permute-start.13
  217.0 23.1 %copy-start.13 = (f32[6,6,128]{2,1,0:T(8,128)S(1)}, f32[6,6,128]{2,1,0:T(8,128)}, u32[]{:S(2)}) copy-start(f32[6,6,128]{2,1,0:T(8,128)} %copy-done.12) | copy-start | bytes 55300
  220.8 5.9 collective-permute-start.18
  226.6 13.4 %collective-permute-start.23 = (f32[1,128,128]{2,1,0:T(8,128)S(1)}, f32[1,128,128]{2,1,0:T(8,128)S(1)}, u32[]{:S(2)}, u32[]{:S(2)}) collective-permute-start(f32[1,128,128]{2,1,0:T(8,128)S(1)} %get-tuple-element.40), channel_id=1, source_target_pairs={{1,0},{2,1},{3,2},{0,3},{5,4},{6,5},{7,6},{4,7},{9,8},{10,9},{11,1... | collective-permute-start | bytes 196616 | tf_op jit(solution)/shard_map/ppermute | solution.py:20
  226.7 13.3 %collective-permute-start.22 = (f32[1,128,128]{2,1,0:T(8,128)S(1)}, f32[1,128,128]{2,1,0:T(8,128)S(1)}, u32[]{:S(2)}, u32[]{:S(2)}) collective-permute-start(f32[1,128,128]{2,1,0:T(8,128)S(1)} %get-tuple-element.42), channel_id=1, source_target_pairs={{0,1},{1,2},{2,3},{3,0},{4,5},{5,6},{6,7},{7,4},{8,9},{9,10},{10,1... | collective-permute-start | bytes 196616 | tf_op jit(solution)/shard_map/ppermute | solution.py:19
  227.2 12.7 %collective-permute-start.20 = (f32[1,128,128]{2,1,0:T(8,128)S(1)}, f32[1,128,128]{2,1,0:T(8,128)S(1)}, u32[]{:S(2)}, u32[]{:S(2)}) collective-permute-start(f32[1,128,128]{2,1,0:T(8,128)S(1)} %get-tuple-element.43), channel_id=1, source_target_pairs={{0,4},{4,8},{8,12},{12,0},{1,5},{5,9},{9,13},{13,1},{2,6},{6,10},{... | collective-permute-start | bytes 196616 | tf_op jit(solution)/shard_map/ppermute | solution.py:19
  227.2 12.8 %collective-permute-start.21 = (f32[1,128,128]{2,1,0:T(8,128)S(1)}, f32[1,128,128]{2,1,0:T(8,128)S(1)}, u32[]{:S(2)}, u32[]{:S(2)}) collective-permute-start(f32[1,128,128]{2,1,0:T(8,128)S(1)} %get-tuple-element.44), channel_id=1, source_target_pairs={{4,0},{8,4},{12,8},{0,12},{5,1},{9,5},{13,9},{1,13},{6,2},{10,6},{... | collective-permute-start | bytes 196616 | tf_op jit(solution)/shard_map/ppermute | solution.py:20
  235.7 4.3 collective-permute-start.19
  283.9 7.8 %collective-permute-start.24 = (f32[1,128,128]{2,1,0:T(8,128)S(1)}, f32[1,128,128]{2,1,0:T(8,128)S(1)}, u32[]{:S(2)}, u32[]{:S(2)}) collective-permute-start(f32[1,128,128]{2,1,0:T(8,128)S(1)} %slice.480), channel_id=1, source_target_pairs={{0,16},{16,0},{1,17},{17,1},{2,18},{18,2},{3,19},{19,3},{4,20},{20... | collective-permute-start | bytes 196616 | tf_op jit(solution)/shard_map/ppermute | solution.py:19
  291.7 10.4 %collective-permute-start.29 = (f32[1,128,128]{2,1,0:T(8,128)S(1)}, f32[1,128,128]{2,1,0:T(8,128)S(1)}, u32[]{:S(2)}, u32[]{:S(2)}) collective-permute-start(f32[1,128,128]{2,1,0:T(8,128)S(1)} %get-tuple-element.34), channel_id=1, source_target_pairs={{1,0},{2,1},{3,2},{0,3},{5,4},{6,5},{7,6},{4,7},{9,8},{10,9},{11,1... | collective-permute-start | bytes 196616 | tf_op jit(solution)/shard_map/ppermute | solution.py:20
  293.5 8.5 %collective-permute-start.28 = (f32[1,128,128]{2,1,0:T(8,128)S(1)}, f32[1,128,128]{2,1,0:T(8,128)S(1)}, u32[]{:S(2)}, u32[]{:S(2)}) collective-permute-start(f32[1,128,128]{2,1,0:T(8,128)S(1)} %get-tuple-element.36), channel_id=1, source_target_pairs={{0,1},{1,2},{2,3},{3,0},{4,5},{5,6},{6,7},{7,4},{8,9},{9,10},{10,1... | collective-permute-start | bytes 196616 | tf_op jit(solution)/shard_map/ppermute | solution.py:19
  293.5 8.4 %collective-permute-start.26 = (f32[1,128,128]{2,1,0:T(8,128)S(1)}, f32[1,128,128]{2,1,0:T(8,128)S(1)}, u32[]{:S(2)}, u32[]{:S(2)}) collective-permute-start(f32[1,128,128]{2,1,0:T(8,128)S(1)} %get-tuple-element.37), channel_id=1, source_target_pairs={{0,4},{4,8},{8,12},{12,0},{1,5},{5,9},{9,13},{13,1},{2,6},{6,10},{... | collective-permute-start | bytes 196616 | tf_op jit(solution)/shard_map/ppermute | solution.py:19
  293.5 8.5 %collective-permute-start.27 = (f32[1,128,128]{2,1,0:T(8,128)S(1)}, f32[1,128,128]{2,1,0:T(8,128)S(1)}, u32[]{:S(2)}, u32[]{:S(2)}) collective-permute-start(f32[1,128,128]{2,1,0:T(8,128)S(1)} %get-tuple-element.38), channel_id=1, source_target_pairs={{4,0},{8,4},{12,8},{0,12},{5,1},{9,5},{13,9},{1,13},{6,2},{10,6},{... | collective-permute-start | bytes 196616 | tf_op jit(solution)/shard_map/ppermute | solution.py:20
  297.7 4.3 collective-permute-start.25
  415.6 4.3 collective-permute-start.30
  420.0 13.4 %collective-permute-start.35 = (f32[1,128,128]{2,1,0:T(8,128)S(1)}, f32[1,128,128]{2,1,0:T(8,128)S(1)}, u32[]{:S(2)}, u32[]{:S(2)}) collective-permute-start(f32[1,128,128]{2,1,0:T(8,128)S(1)} %get-tuple-element.28), channel_id=1, source_target_pairs={{1,0},{2,1},{3,2},{0,3},{5,4},{6,5},{7,6},{4,7},{9,8},{10,9},{11,1... | collective-permute-start | bytes 196616 | tf_op jit(solution)/shard_map/ppermute | solution.py:20
  420.1 13.3 %collective-permute-start.34 = (f32[1,128,128]{2,1,0:T(8,128)S(1)}, f32[1,128,128]{2,1,0:T(8,128)S(1)}, u32[]{:S(2)}, u32[]{:S(2)}) collective-permute-start(f32[1,128,128]{2,1,0:T(8,128)S(1)} %get-tuple-element.30), channel_id=1, source_target_pairs={{0,1},{1,2},{2,3},{3,0},{4,5},{5,6},{6,7},{7,4},{8,9},{9,10},{10,1... | collective-permute-start | bytes 196616 | tf_op jit(solution)/shard_map/ppermute | solution.py:19
  420.6 12.7 %collective-permute-start.32 = (f32[1,128,128]{2,1,0:T(8,128)S(1)}, f32[1,128,128]{2,1,0:T(8,128)S(1)}, u32[]{:S(2)}, u32[]{:S(2)}) collective-permute-start(f32[1,128,128]{2,1,0:T(8,128)S(1)} %get-tuple-element.31), channel_id=1, source_target_pairs={{0,4},{4,8},{8,12},{12,0},{1,5},{5,9},{9,13},{13,1},{2,6},{6,10},{... | collective-permute-start | bytes 196616 | tf_op jit(solution)/shard_map/ppermute | solution.py:19
  420.6 12.8 %collective-permute-start.33 = (f32[1,128,128]{2,1,0:T(8,128)S(1)}, f32[1,128,128]{2,1,0:T(8,128)S(1)}, u32[]{:S(2)}, u32[]{:S(2)}) collective-permute-start(f32[1,128,128]{2,1,0:T(8,128)S(1)} %get-tuple-element.32), channel_id=1, source_target_pairs={{4,0},{8,4},{12,8},{0,12},{5,1},{9,5},{13,9},{1,13},{6,2},{10,6},{... | collective-permute-start | bytes 196616 | tf_op jit(solution)/shard_map/ppermute | solution.py:20
  429.0 4.3 collective-permute-start.31
  470.8 21.7 %copy-start.20 = (f32[6,128,128]{2,1,0:T(8,128)S(1)}, f32[6,128,128]{2,1,0:T(8,128)}, u32[]{:S(2)}) copy-start(f32[6,128,128]{2,1,0:T(8,128)} %copy-done.19) | copy-start | bytes 1179652
  472.6 8.4 %collective-permute-start.36 = (f32[1,128,128]{2,1,0:T(8,128)S(1)}, f32[1,128,128]{2,1,0:T(8,128)S(1)}, u32[]{:S(2)}, u32[]{:S(2)}) collective-permute-start(f32[1,128,128]{2,1,0:T(8,128)S(1)} %slice.494), channel_id=1, source_target_pairs={{0,16},{16,0},{1,17},{17,1},{2,18},{18,2},{3,19},{19,3},{4,20},{20... | collective-permute-start | bytes 196616 | tf_op jit(solution)/shard_map/ppermute | solution.py:19
  481.0 10.3 %collective-permute-start.41 = (f32[1,128,128]{2,1,0:T(8,128)S(1)}, f32[1,128,128]{2,1,0:T(8,128)S(1)}, u32[]{:S(2)}, u32[]{:S(2)}) collective-permute-start(f32[1,128,128]{2,1,0:T(8,128)S(1)} %get-tuple-element.22), channel_id=1, source_target_pairs={{1,0},{2,1},{3,2},{0,3},{5,4},{6,5},{7,6},{4,7},{9,8},{10,9},{11,1... | collective-permute-start | bytes 196616 | tf_op jit(solution)/shard_map/ppermute | solution.py:20
  482.7 8.5 %collective-permute-start.40 = (f32[1,128,128]{2,1,0:T(8,128)S(1)}, f32[1,128,128]{2,1,0:T(8,128)S(1)}, u32[]{:S(2)}, u32[]{:S(2)}) collective-permute-start(f32[1,128,128]{2,1,0:T(8,128)S(1)} %get-tuple-element.24), channel_id=1, source_target_pairs={{0,1},{1,2},{2,3},{3,0},{4,5},{5,6},{6,7},{7,4},{8,9},{9,10},{10,1... | collective-permute-start | bytes 196616 | tf_op jit(solution)/shard_map/ppermute | solution.py:19
  482.7 8.4 %collective-permute-start.38 = (f32[1,128,128]{2,1,0:T(8,128)S(1)}, f32[1,128,128]{2,1,0:T(8,128)S(1)}, u32[]{:S(2)}, u32[]{:S(2)}) collective-permute-start(f32[1,128,128]{2,1,0:T(8,128)S(1)} %get-tuple-element.25), channel_id=1, source_target_pairs={{0,4},{4,8},{8,12},{12,0},{1,5},{5,9},{9,13},{13,1},{2,6},{6,10},{... | collective-permute-start | bytes 196616 | tf_op jit(solution)/shard_map/ppermute | solution.py:19
  482.7 8.5 %collective-permute-start.39 = (f32[1,128,128]{2,1,0:T(8,128)S(1)}, f32[1,128,128]{2,1,0:T(8,128)S(1)}, u32[]{:S(2)}, u32[]{:S(2)}) collective-permute-start(f32[1,128,128]{2,1,0:T(8,128)S(1)} %get-tuple-element.26), channel_id=1, source_target_pairs={{4,0},{8,4},{12,8},{0,12},{5,1},{9,5},{13,9},{1,13},{6,2},{10,6},{... | collective-permute-start | bytes 196616 | tf_op jit(solution)/shard_map/ppermute | solution.py:20
  486.9 4.3 collective-permute-start.37
  606.1 4.3 collective-permute-start.42
  610.4 13.4 %collective-permute-start.47 = (f32[1,128,128]{2,1,0:T(8,128)S(1)}, f32[1,128,128]{2,1,0:T(8,128)S(1)}, u32[]{:S(2)}, u32[]{:S(2)}) collective-permute-start(f32[1,128,128]{2,1,0:T(8,128)S(1)} %get-tuple-element.16), channel_id=1, source_target_pairs={{1,0},{2,1},{3,2},{0,3},{5,4},{6,5},{7,6},{4,7},{9,8},{10,9},{11,1... | collective-permute-start | bytes 196616 | tf_op jit(solution)/shard_map/ppermute | solution.py:20
  610.5 13.3 %collective-permute-start.46 = (f32[1,128,128]{2,1,0:T(8,128)S(1)}, f32[1,128,128]{2,1,0:T(8,128)S(1)}, u32[]{:S(2)}, u32[]{:S(2)}) collective-permute-start(f32[1,128,128]{2,1,0:T(8,128)S(1)} %get-tuple-element.18), channel_id=1, source_target_pairs={{0,1},{1,2},{2,3},{3,0},{4,5},{5,6},{6,7},{7,4},{8,9},{9,10},{10,1... | collective-permute-start | bytes 196616 | tf_op jit(solution)/shard_map/ppermute | solution.py:19
  611.0 12.7 %collective-permute-start.44 = (f32[1,128,128]{2,1,0:T(8,128)S(1)}, f32[1,128,128]{2,1,0:T(8,128)S(1)}, u32[]{:S(2)}, u32[]{:S(2)}) collective-permute-start(f32[1,128,128]{2,1,0:T(8,128)S(1)} %get-tuple-element.19), channel_id=1, source_target_pairs={{0,4},{4,8},{8,12},{12,0},{1,5},{5,9},{9,13},{13,1},{2,6},{6,10},{... | collective-permute-start | bytes 196616 | tf_op jit(solution)/shard_map/ppermute | solution.py:19
  611.0 12.8 %collective-permute-start.45 = (f32[1,128,128]{2,1,0:T(8,128)S(1)}, f32[1,128,128]{2,1,0:T(8,128)S(1)}, u32[]{:S(2)}, u32[]{:S(2)}) collective-permute-start(f32[1,128,128]{2,1,0:T(8,128)S(1)} %get-tuple-element.20), channel_id=1, source_target_pairs={{4,0},{8,4},{12,8},{0,12},{5,1},{9,5},{13,9},{1,13},{6,2},{10,6},{... | collective-permute-start | bytes 196616 | tf_op jit(solution)/shard_map/ppermute | solution.py:20
  619.5 4.3 collective-permute-start.43
  661.0 21.8 %copy-start.22 = (f32[6,128,128]{2,1,0:T(8,128)S(1)}, f32[6,128,128]{2,1,0:T(8,128)}, u32[]{:S(2)}) copy-start(f32[6,128,128]{2,1,0:T(8,128)} %copy-done.21) | copy-start | bytes 1179652
  662.8 63.2 %copy-start.10 = (f32[6,128,128]{2,1,0:T(8,128)S(1)}, f32[6,128,128]{2,1,0:T(8,128)}, u32[]{:S(2)}) copy-start(f32[6,128,128]{2,1,0:T(8,128)} %get-tuple-element.69) | copy-start | bytes 1179652
  662.9 63.2 %copy-start.89 = (f32[128]{0:T(128)S(1)}, f32[128]{0:T(128)}, u32[]{:S(2)}) copy-start(f32[128]{0:T(128)} %copy-done.88) | copy-start | bytes 1540
  662.9 63.2 %copy-start.91 = (f32[128]{0:T(128)S(1)}, f32[128]{0:T(128)}, u32[]{:S(2)}) copy-start(f32[128]{0:T(128)} %copy-done.90) | copy-start | bytes 1540
  662.9 8.4 %collective-permute-start.48 = (f32[1,128,128]{2,1,0:T(8,128)S(1)}, f32[1,128,128]{2,1,0:T(8,128)S(1)}, u32[]{:S(2)}, u32[]{:S(2)}) collective-permute-start(f32[1,128,128]{2,1,0:T(8,128)S(1)} %slice.509), channel_id=1, source_target_pairs={{0,16},{16,0},{1,17},{17,1},{2,18},{18,2},{3,19},{19,3},{4,20},{20... | collective-permute-start | bytes 196616 | tf_op jit(solution)/shard_map/ppermute | solution.py:19
  671.3 10.3 %collective-permute-start.53 = (f32[1,128,128]{2,1,0:T(8,128)S(1)}, f32[1,128,128]{2,1,0:T(8,128)S(1)}, u32[]{:S(2)}, u32[]{:S(2)}) collective-permute-start(f32[1,128,128]{2,1,0:T(8,128)S(1)} %get-tuple-element.10), channel_id=1, source_target_pairs={{1,0},{2,1},{3,2},{0,3},{5,4},{6,5},{7,6},{4,7},{9,8},{10,9},{11,1... | collective-permute-start | bytes 196616 | tf_op jit(solution)/shard_map/ppermute | solution.py:20
  673.0 8.5 %collective-permute-start.52 = (f32[1,128,128]{2,1,0:T(8,128)S(1)}, f32[1,128,128]{2,1,0:T(8,128)S(1)}, u32[]{:S(2)}, u32[]{:S(2)}) collective-permute-start(f32[1,128,128]{2,1,0:T(8,128)S(1)} %get-tuple-element.12), channel_id=1, source_target_pairs={{0,1},{1,2},{2,3},{3,0},{4,5},{5,6},{6,7},{7,4},{8,9},{9,10},{10,1... | collective-permute-start | bytes 196616 | tf_op jit(solution)/shard_map/ppermute | solution.py:19
  673.0 8.4 %collective-permute-start.50 = (f32[1,128,128]{2,1,0:T(8,128)S(1)}, f32[1,128,128]{2,1,0:T(8,128)S(1)}, u32[]{:S(2)}, u32[]{:S(2)}) collective-permute-start(f32[1,128,128]{2,1,0:T(8,128)S(1)} %get-tuple-element.13), channel_id=1, source_target_pairs={{0,4},{4,8},{8,12},{12,0},{1,5},{5,9},{9,13},{13,1},{2,6},{6,10},{... | collective-permute-start | bytes 196616 | tf_op jit(solution)/shard_map/ppermute | solution.py:19
  673.0 8.5 %collective-permute-start.51 = (f32[1,128,128]{2,1,0:T(8,128)S(1)}, f32[1,128,128]{2,1,0:T(8,128)S(1)}, u32[]{:S(2)}, u32[]{:S(2)}) collective-permute-start(f32[1,128,128]{2,1,0:T(8,128)S(1)} %get-tuple-element.14), channel_id=1, source_target_pairs={{4,0},{8,4},{12,8},{0,12},{5,1},{9,5},{13,9},{1,13},{6,2},{10,6},{... | collective-permute-start | bytes 196616 | tf_op jit(solution)/shard_map/ppermute | solution.py:20
  677.2 4.3 collective-permute-start.49
  (83 other events, 478.9 us)
